TPU v7x, 32 devices: a whole 2x2x4 slice. The times are simulated.
32 devices in a mesh: visit: 8 (over y, x, core), sky: 4 (over z).
Axes of the slice: x: 2, y: 2, z: 4, core: 2. Of those that a mesh axis runs over, the one named last changes fastest.
Arguments:
- science: float32 [8, 16, 128, 128], P('visit', 'sky'), may hold values from -6 to 6
- coef_first: float32 [8, 16, 3, 49], P('visit', 'sky'), may hold values from -4 to 4
- coef_second: float32 [8, 16, 3, 49], P('visit', 'sky'), may hold values from -4 to 4
- weight: float32 [8, 16], P('visit', 'sky'), may hold values from 0.3 to 3
- slot_tile: int32 [8, 16], P('visit', 'sky'), may hold values from 0 to 3, as said below
- offsets: int32 [8, 16, 2], P('visit', 'sky'), may hold values from 0 to 128
- counts: int32 [8, 4], P('visit', 'sky'), may hold values from 3 to 4, as said below
- tile_place: int32 [4], replicated, may hold values from 0 to 3, as said below
Outputs:
- template: float32 [4, 256, 256], P('sky')
- difference: float32 [8, 16, 128, 128], P('visit', 'sky')
Inputs may be any that keep to these rules, and one draw needn't show every extreme that they name: `slot_tile`: among the usable slots of one device's list at most 2 name tiles of one owner; in every visit the tile of some owner gets exactly 2 usable slots from every device of the sky axis. A permutation: tile t is owned by the device of sky index tile_place[t]. The first counts[v, s] slots of a device's list are usable; in every visit some device has all 4 usable.
All inputs are finite; a program needn't handle non-finite values.
Results may differ from a plain program's by a relative error of at most 0.00011.
Values sent between devices are 32-bit elements; how exact they have to be, the bound alone decides.
No kernel may reach another device: no remote copies, remote signals or barrier semaphores. Data moves between devices by JAX's collectives and lax.ppermute only.
A program may use at most 64 MiB of HBM per device.

v0:
```python
import jax
import jax.numpy as jnp
from jax import lax
from jax.sharding import PartitionSpec as P

TILE = 256
TAPS = 21
PROFILES = 7
WIDTHS = (1.0, 1.0, 1.0, 2.5, 2.5, 2.5, 5.0)
POWERS = (0, 1, 2, 0, 1, 2, 0)
PRECISE = lax.Precision.HIGHEST


def profile_filters(side):
    reach = (TAPS - 1) // 2
    places = jnp.arange(side).astype(jnp.float32)
    spacing = places[None, :] - places[:, None]
    support = jnp.arange(TAPS).astype(jnp.float32) - reach
    stacked = []
    for number in range(PROFILES):
        sample = support ** POWERS[number] * jnp.exp(
            -support * support / (2.0 * WIDTHS[number] ** 2)
        )
        norming = jnp.sqrt(jnp.sum(sample * sample))
        values = spacing ** POWERS[number] * jnp.exp(
            -spacing * spacing / (2.0 * WIDTHS[number] ** 2)
        )
        stacked.append(jnp.where(jnp.abs(spacing) <= reach, values / norming, 0.0))
    return jnp.stack(stacked)


def positions(side):
    places = jnp.arange(side).astype(jnp.float32)
    return (2.0 * places - (side - 1)) / (side - 1)


def kernel_pass(block, coeffs, filters, spread):
    across_x = jnp.einsum("yw,ixw->iyx", block, filters, precision=PRECISE)
    layout = coeffs.reshape(3, PROFILES, PROFILES)
    plain = jnp.einsum("ij,jab->iab", layout[0], filters, precision=PRECISE)
    along = jnp.einsum("ij,jab->iab", layout[2], filters, precision=PRECISE) * spread[None, :, None]
    sideways = jnp.einsum("ij,jab->iab", layout[1], filters, precision=PRECISE)
    steady = jnp.einsum("iab,ibx->ax", plain + along, across_x, precision=PRECISE)
    varying = jnp.einsum("iab,ibx->ax", sideways, across_x, precision=PRECISE)
    return steady + varying * spread[None, :]


def body(science, coef_first, coef_second, weight, slot_tile, offsets, counts, tile_place):
    slots = science.shape[1]
    side = science.shape[2]
    owners_count = lax.axis_size("sky")
    capacity = max(2, (slots + owners_count - 1) // owners_count)
    buffer_slots = owners_count * capacity
    filters = profile_filters(side)
    spread = positions(side)
    listed = jnp.arange(slots)
    usable = listed < counts[0, 0]
    tile_ids = jnp.arange(tile_place.shape[0])
    owners = jnp.sum(
        jnp.where(slot_tile[0][:, None] == tile_ids[None, :], tile_place[None, :], 0), axis=1
    )
    convolved = lax.map(
        lambda operands: kernel_pass(operands[0], operands[1], filters, spread),
        (science[0], coef_first[0]),
    )
    sharing = (
        (owners[:, None] == owners[None, :]) & usable[None, :] & (listed[None, :] < listed[:, None])
    )
    earlier = jnp.sum(sharing.astype(jnp.int32), axis=1)
    target = jnp.where(usable, owners * capacity + earlier, -1)
    routing = (target[None, :] == jnp.arange(buffer_slots)[:, None]).astype(jnp.float32)
    packed = jnp.dot(routing, convolved.reshape(slots, side * side), precision=PRECISE).reshape(
        buffer_slots, side, side
    )
    sent_weight = jnp.dot(routing, weight[0], precision=PRECISE)
    sent_corner = jnp.dot(routing, offsets[0].astype(jnp.float32), precision=PRECISE)
    arrived, arrived_weight, arrived_corner = (
        lax.all_to_all(packed, "sky", split_axis=0, concat_axis=0, tiled=True),
        lax.all_to_all(sent_weight, "sky", split_axis=0, concat_axis=0, tiled=True),
        lax.all_to_all(sent_corner, "sky", split_axis=0, concat_axis=0, tiled=True),
    )
    corners = arrived_corner.astype(jnp.int32)

    def place_block(position, totals):
        weighted, coverage = totals
        corner_top = corners[position, 0]
        corner_left = corners[position, 1]
        block_weight = arrived_weight[position]
        region = lax.dynamic_slice(weighted, (corner_top, corner_left), (side, side))
        weighted = lax.dynamic_update_slice(
            weighted, region + block_weight * arrived[position], (corner_top, corner_left)
        )
        region = lax.dynamic_slice(coverage, (corner_top, corner_left), (side, side))
        coverage = lax.dynamic_update_slice(
            coverage, region + block_weight, (corner_top, corner_left)
        )
        return (weighted, coverage)

    empty = jnp.zeros((TILE, TILE), jnp.float32)
    weighted, coverage = lax.fori_loop(0, buffer_slots, place_block, (empty, empty))
    weighted, coverage = lax.psum((weighted, coverage), "visit")
    template = weighted / (coverage + 1.0)
    cut_back = jax.vmap(
        lambda corner: lax.dynamic_slice(template, (corner[0], corner[1]), (side, side))
    )(corners)
    returned = lax.all_to_all(cut_back, "sky", split_axis=0, concat_axis=0, tiled=True)
    cutouts = jnp.dot(
        routing.T, returned.reshape(buffer_slots, side * side), precision=PRECISE
    ).reshape(slots, side, side)
    matched = lax.map(
        lambda operands: kernel_pass(operands[0], operands[1], filters, spread),
        (cutouts, coef_second[0]),
    )
    difference = jnp.where(usable[:, None, None], science[0] - matched, 0.0)
    return (template[None], difference[None])


def solution(mesh):
    in_specs = (
        P("visit", "sky", None, None),
        P("visit", "sky", None, None),
        P("visit", "sky", None, None),
        P("visit", "sky"),
        P("visit", "sky"),
        P("visit", "sky", None),
        P("visit", "sky"),
        P(),
    )
    out_specs = (P("sky", None, None), P("visit", "sky", None, None))
    return jax.shard_map(body, mesh=mesh, in_specs=in_specs, out_specs=out_specs, check_vma=False)
```

profile of v0, /device:TPU:0, one launch (start us, length us, event | category | flops | bytes accessed | tf_op | source)
XLA Modules:
  0.0 270.1 jit_solution(13443177923790171623)
XLA Ops:
  9.1 0.7 copy.57
  9.8 6.3 %all-to-all-start.1 = ((f32[4,2,1]{1,2,0:T(1,128)}), f32[4,2,1]{1,2,0:T(1,128)S(1)}, u32[]{:S(2)}, u32[]{:S(2)}) async-start(f32[4,2,1]{1,2,0:T(1,128)} %copy.57), calls=%async_computation.1 | async-start | bytes 4096 | tf_op jit(solution)/shard_map/all_to_all | solution.py:79
  16.8 0.7 multiply_reduce_fusion.5
  19.4 0.7 multiply_reduce_fusion.1
  26.1 0.7 stack.2
  26.9 0.9 copy-done.4
  27.8 15.7 %while.42 = (s32[]{:T(128)}, f32[4,128,128]{2,1,0:T(8,128)S(1)}, f32[4,3,49]{2,1,0:T(4,128)S(1)}, f32[7,128,128]{2,0,1:T(8,128)S(1)}, f32[4,128,128]{2,1,0:T(8,128)S(1)}, /*index=5*/s32[]{:T(128)}) while((s32[]{:T(128)}, f32[4,128,128]{2,1,0:T(8,128)S(1)}, f32[4,3,49]{2,1,0:T(4,128)S(1)}, ...), condition=%wide.region_10.11_spmd.clone.clone, body=%wide.region_9.10_spmd.clone.clone.sunk | while | flops 557646336 | bytes 6362725 | solution.py:62
  44.2 0.7 fusion.28
  45.0 5.1 %all-to-all-start = ((f32[4,2,2]{2,1,0:T(2,128)}), f32[4,2,2]{2,1,0:T(2,128)S(1)}, u32[]{:S(2)}, u32[]{:S(2)}) async-start(f32[4,2,2]{2,1,0:T(2,128)} %fusion.28), calls=%async_computation | async-start | bytes 8192 | tf_op jit(solution)/shard_map/all_to_all | solution.py:80
  50.1 0.9 copy.59
  51.0 4.7 %all-to-all-done = f32[4,2,2]{2,1,0:T(2,128)S(1)} async-done(((f32[4,2,2]{2,1,0:T(2,128)}), f32[4,2,2]{2,1,0:T(2,128)S(1)}, u32[]{:S(2)}, u32[]{:S(2)}) %all-to-all-start) | async-done | bytes 96 | tf_op jit(solution)/shard_map/all_to_all | solution.py:80
  55.6 3.5 %all-to-all-start.2 = ((f32[8,128,128]{2,1,0:T(8,128)}), f32[8,128,128]{2,1,0:T(8,128)S(1)}, u32[]{:S(2)}, u32[]{:S(2)}) async-start(f32[8,128,128]{2,1,0:T(8,128)} %copy.59), calls=%async_computation.2 | async-start | bytes 1048576 | tf_op jit(solution)/shard_map/all_to_all | solution.py:78
  59.7 0.7 reduce.27
  60.7 11.1 %all-to-all-done.2 = f32[8,128,128]{2,1,0:T(8,128)S(1)} async-done(((f32[8,128,128]{2,1,0:T(8,128)}), f32[8,128,128]{2,1,0:T(8,128)S(1)}, u32[]{:S(2)}, u32[]{:S(2)}) %all-to-all-start.2) | async-done | bytes 524320 | tf_op jit(solution)/shard_map/all_to_all | solution.py:78
  71.9 77.3 %while.40 = (s32[]{:T(128)}, f32[256,256]{1,0:T(8,128)S(1)}, f32[256,256]{1,0:T(8,128)S(1)}, s32[8,2]{0,1:T(2,128)S(1)}, f32[8]{0:T(128)S(1)}, /*index=5*/f32[8,...) while((s32[]{:T(128)}, f32[256,256]{1,0:T(8,128)S(1)}, f32[256,256]{1,0:T(8,128)S(1)}, ...), condition=%wide.region_12.13_spmd, body=%wide.region_11.12_spmd.sunk | while | flops 49160 | bytes 591569 | solution.py:100
  71.9 0.7 constant_dynamic-slice_fusion.11
  77.2 0.8 bitcast_add_fusion.2
  78.0 2.0 dynamic_update_slice.32
  79.9 2.0 dynamic_update_slice.31
  81.9 0.7 constant_dynamic-slice_fusion.11
  87.2 0.8 bitcast_add_fusion.2
  88.0 1.9 dynamic_update_slice.32
  89.9 1.9 dynamic_update_slice.31
  91.9 0.7 constant_dynamic-slice_fusion.11
  97.2 0.8 bitcast_add_fusion.2
  97.9 2.0 dynamic_update_slice.32
  99.9 2.0 dynamic_update_slice.31
  101.9 0.7 constant_dynamic-slice_fusion.11
  107.2 0.8 bitcast_add_fusion.2
  107.9 1.7 dynamic_update_slice.32
  109.6 1.7 dynamic_update_slice.31
  111.3 0.7 constant_dynamic-slice_fusion.11
  116.6 0.8 bitcast_add_fusion.2
  117.3 1.9 dynamic_update_slice.32
  119.2 1.9 dynamic_update_slice.31
  121.1 0.7 constant_dynamic-slice_fusion.11
  126.4 0.8 bitcast_add_fusion.2
  127.1 1.7 dynamic_update_slice.32
  128.8 1.7 dynamic_update_slice.31
  130.5 0.7 constant_dynamic-slice_fusion.11
  135.8 0.8 bitcast_add_fusion.2
  136.5 1.7 dynamic_update_slice.32
  138.2 1.7 dynamic_update_slice.31
  139.9 0.7 constant_dynamic-slice_fusion.11
  145.1 0.8 bitcast_add_fusion.2
  145.9 1.7 dynamic_update_slice.32
  147.6 1.7 dynamic_update_slice.31
  149.3 0.7 copy-done.1
  150.1 54.8 %all-reduce.3.cloned.1.call-done = (f32[256,256]{1,0:T(8,128)}, f32[256,256]{1,0:T(8,128)}) async-done(((f32[256,256]{1,0:T(8,128)}, f32[256,256]{1,0:T(8,128)}), (f32[256,256]{1,0:T(8,128)}, f32[256,256]{1,0:T(8,128)})) %all-reduce.3.cloned.1.call-update) | async-done | bytes 524304 | tf_op jit(solution)/shard_map/psum | solution.py:101
  204.9 1.1 add_divide_fusion
  205.9 20.8 %while.41 = (s32[]{:T(128)}, f32[256,256]{1,0:T(8,128)S(1)}, s32[8,2]{0,1:T(2,128)S(1)}, f32[8,128,128]{2,1,0:T(8,128)}, s32[]{:T(128)}) while((s32[]{:T(128)}, f32[256,256]{1,0:T(8,128)S(1)}, s32[8,2]{0,1:T(2,128)S(1)}, f32[8,128,128]{2,1,0:T(8,128)}, s32[]{:T(128)}) %tuple.118), condition=%wide.while_cond, body=%wide.while_body.sunk | while | flops 2 | bytes 132705 | solution.py:104
  206.6 2.0 bitcast_dynamic-update-slice_fusion.2
  209.2 2.0 bitcast_dynamic-update-slice_fusion.2
  211.8 2.0 bitcast_dynamic-update-slice_fusion.2
  214.4 2.0 bitcast_dynamic-update-slice_fusion.2
  217.0 2.0 bitcast_dynamic-update-slice_fusion.2
  219.5 2.0 bitcast_dynamic-update-slice_fusion.2
  222.2 2.0 bitcast_dynamic-update-slice_fusion.2
  224.8 2.0 bitcast_dynamic-update-slice_fusion.2
  226.8 0.7 copy-done.3
  227.5 4.6 %all-to-all-start.3 = ((f32[8,128,128]{2,1,0:T(8,128)}), f32[8,128,128]{2,1,0:T(8,128)S(1)}, u32[]{:S(2)}, u32[]{:S(2)}) async-start(f32[8,128,128]{2,1,0:T(8,128)} %get-tuple-element.193), calls=%async_computation.3 | async-start | bytes 1048576 | tf_op jit(solution)/shard_map/all_to_all | solution.py:106
  232.0 13.8 %all-to-all-done.3 = f32[8,128,128]{2,1,0:T(8,128)S(1)} async-done(((f32[8,128,128]{2,1,0:T(8,128)}), f32[8,128,128]{2,1,0:T(8,128)S(1)}, u32[]{:S(2)}, u32[]{:S(2)}) %all-to-all-start.3) | async-done | bytes 524320 | tf_op jit(solution)/shard_map/all_to_all | solution.py:106
  246.5 16.0 %while.43 = (s32[]{:T(128)}, f32[4,128,128]{2,1,0:T(8,128)S(1)}, f32[4,3,49]{2,1,0:T(4,128)S(1)}, f32[7,128,128]{2,0,1:T(8,128)S(1)}, f32[4,128,128]{2,0,1:T(4,128)S(1)}, /*index=5*/s32[]{:T(128)}) while((s32[]{:T(128)}, f32[4,128,128]{2,1,0:T(8,128)S(1)}, f32[4,3,49]{2,1,0:T(4,128)S(1)}, ...), condition=%wide.region_16.17_spmd.clone.clone, body=%wide.region_15.16_spmd.clone.clone.sunk | while | flops 557646336 | bytes 6428261 | solution.py:110
  262.5 0.8 select_bitcast_fusion
  (175 shorter events, 48.2 us)
Async XLA Ops:
  7.2 1.8 copy-start
  7.8 0.7 copy-start.8
  7.9 0.7 copy-start.9
  9.8 35.1 %all-to-all-start.1 = ((f32[4,2,1]{1,2,0:T(1,128)}), f32[4,2,1]{1,2,0:T(1,128)S(1)}, u32[]{:S(2)}, u32[]{:S(2)}) async-start(f32[4,2,1]{1,2,0:T(1,128)} %copy.57), calls=%async_computation.1 | async-start | bytes 4096 | tf_op jit(solution)/shard_map/all_to_all | solution.py:79
  22.7 2.7 %copy-start.5 = (f32[1,4,3,49]{3,1,2,0:T(4,128)S(1)}, f32[1,4,3,49]{3,1,2,0:T(4,128)}, u32[]{:S(2)}) copy-start(f32[1,4,3,49]{3,1,2,0:T(4,128)} %param.15) | copy-start | bytes 7060
  26.8 1.0 copy-start.4
  43.5 0.7 copy-start.7
  45.0 10.7 %all-to-all-start = ((f32[4,2,2]{2,1,0:T(2,128)}), f32[4,2,2]{2,1,0:T(2,128)S(1)}, u32[]{:S(2)}, u32[]{:S(2)}) async-start(f32[4,2,2]{2,1,0:T(2,128)} %fusion.28), calls=%async_computation | async-start | bytes 8192 | tf_op jit(solution)/shard_map/all_to_all | solution.py:80
  55.6 16.2 %all-to-all-start.2 = ((f32[8,128,128]{2,1,0:T(8,128)}), f32[8,128,128]{2,1,0:T(8,128)S(1)}, u32[]{:S(2)}, u32[]{:S(2)}) async-start(f32[8,128,128]{2,1,0:T(8,128)} %copy.59), calls=%async_computation.2 | async-start | bytes 1048576 | tf_op jit(solution)/shard_map/all_to_all | solution.py:78
  59.1 145.8 %all-reduce.3.cloned.1.call-start = ((), (), s32[]{:S(2)}) async-start(), calls=%async_computation.4 | async-start | bytes 1048576 | tf_op jit(solution)/shard_map/psum | solution.py:101
  149.2 0.7 copy-start.1
  149.3 0.8 copy-start.2
  226.8 0.7 copy-start.3
  226.8 5.3 %copy-start.6 = (f32[1,4,3,49]{3,1,2,0:T(4,128)S(1)}, f32[1,4,3,49]{3,1,2,0:T(4,128)}, u32[]{:S(2)}) copy-start(f32[1,4,3,49]{3,1,2,0:T(4,128)} %param.16) | copy-start | bytes 7060
  227.5 18.3 %all-to-all-start.3 = ((f32[8,128,128]{2,1,0:T(8,128)}), f32[8,128,128]{2,1,0:T(8,128)S(1)}, u32[]{:S(2)}, u32[]{:S(2)}) async-start(f32[8,128,128]{2,1,0:T(8,128)} %get-tuple-element.193), calls=%async_computation.3 | async-start | bytes 1048576 | tf_op jit(solution)/shard_map/all_to_all | solution.py:106
Sparse Core Ops, SparseCore 0:
  150.2 54.6 all-reduce.2
where the time goes:
time: 271 us; the launch traced here: 270 us
  waiting for transfers between devices  84.3 us (31%)
  local copies, waits for them, and re-layouts  68.5 us (25%)
  loops' own time  33 us (12%)
  matrix products  30.9 us (11%)
  between operations  19.6 us (7%)
  starting transfers between devices  19.5 us (7%)
  other arithmetic  14.3 us (5%)
    psum x1, waiting for transfers between devices, body(): weighted, coverage = lax.psum((weighted, coverage), 'visit')  54.8 us
    another operation x1, loops' own time, body(): lax.fori_loop(0, buffer_slots, place_block, (empty, empty))  32.4 us
    gather x24, local copies, waits for them, and re-layouts  20.8 us
    dynamic_update_slice x8, local copies, waits for them, and re-layouts, place_block(): lax.dynamic_update_slice(coverage, region + block_weight, (corner_top, co...  14.4 us
    dynamic_update_slice x8, local copies, waits for them, and re-layouts, place_block(): lax.dynamic_update_slice(weighted, region + block_weight * arrived[positi...  14.4 us
    all_to_all x1, waiting for transfers between devices, body(): lax.all_to_all(cut_back, 'sky', split_axis=0, concat_axis=0, tiled=True)  13.8 us
    all_to_all x1, waiting for transfers between devices, body(): lax.all_to_all(packed, 'sky', split_axis=0, concat_axis=0, tiled=True)  11.1 us
    all_to_all x1, starting transfers between devices, body(): lax.all_to_all(sent_weight, 'sky', split_axis=0, concat_axis=0, tiled=True)  6.35 us
  transfers between devices with their start and end apart: 5, of which 4 were waited for; matrix products, arithmetic and copies ran while one was open for 9% of the time, Pallas kernels for 0%

commit v1 on v0

--- a/solution.py
+++ b/solution.py
@@ -1,3 +1,4 @@
+import functools
 import jax
 import jax.numpy as jnp
 from jax import lax
@@ -9,6 +10,29 @@
 WIDTHS = (1.0, 1.0, 1.0, 2.5, 2.5, 2.5, 5.0)
 POWERS = (0, 1, 2, 0, 1, 2, 0)
 PRECISE = lax.Precision.HIGHEST
+
+
+def compute_columns(matrix, ax_name):
+    mid_arr, low = (lax.axis_size(ax_name), lax.axis_index(ax_name))
+    passed = matrix.shape[0] // mid_arr
+    t1 = list(matrix.shape)
+    t1[0] = passed
+    far_arr = t1[0]
+    t1[0] = far_arr * mid_arr
+    aux = jnp.zeros(t1, matrix.dtype)
+    for i0 in range(mid_arr):
+        item_now = lax.dynamic_slice_in_dim(matrix, (low ^ i0) * passed, passed, axis=0)
+        if i0:
+            item_now = lax.ppermute(
+                item_now,
+                axis_name=ax_name,
+                perm=list(map(lambda jj: (jj, jj ^ i0), range(mid_arr))),
+            )
+        aux = lax.dynamic_update_slice_in_dim(aux, item_now, (low ^ i0) * far_arr, axis=0)
+    return aux
+
+
+deliver_copies = functools.partial(compute_columns, ax_name="sky")
 
 
 def profile_filters(side):
@@ -75,7 +99,7 @@
     sent_weight = jnp.dot(routing, weight[0], precision=PRECISE)
     sent_corner = jnp.dot(routing, offsets[0].astype(jnp.float32), precision=PRECISE)
     arrived, arrived_weight, arrived_corner = (
-        lax.all_to_all(packed, "sky", split_axis=0, concat_axis=0, tiled=True),
+        deliver_copies(packed),
         lax.all_to_all(sent_weight, "sky", split_axis=0, concat_axis=0, tiled=True),
         lax.all_to_all(sent_corner, "sky", split_axis=0, concat_axis=0, tiled=True),
     )

time: 271 us -> 263 us (0.970)
  waiting for transfers between devices: 84.3 us -> 77.2 us
    all_to_all x1 -> x0, waiting for transfers between devices: 11.1 us -> none  [body(): lax.all_to_all(packed, 'sky', split_axis=0, concat_axis=0, tiled=True)]
    ppermute x0 -> x3, starting transfers between devices: none -> 5.71 us  [compute_columns(): lax.ppermute(item_now, axis_name=ax_name, perm=list(map(lambda jj: (jj, j...]
    all_to_all x1, waiting for transfers between devices: 0.01 us -> 4.29 us  [body(): lax.all_to_all(sent_weight, 'sky', split_axis=0, concat_axis=0, tiled=True)]
    all_to_all x1 -> x0, starting transfers between devices: 3.47 us -> none  [body(): lax.all_to_all(packed, 'sky', split_axis=0, concat_axis=0, tiled=True)]
  transfers between devices with their start and end apart: 5 -> 7, of which waited for: 4 -> 4; matrix products, arithmetic and copies ran while one was open for 9% -> 1% of each run, Pallas kernels for 0% -> 0%
where the time goes in v1:
time: 263 us; the launch traced here: 262 us
  waiting for transfers between devices  77.2 us (29%)
  local copies, waits for them, and re-layouts  68.6 us (26%)
  loops' own time  32 us (12%)
  matrix products  30.9 us (12%)
  between operations  19.7 us (7%)
  starting transfers between devices  19.1 us (7%)
  other arithmetic  14.3 us (5%)
    psum x1, waiting for transfers between devices, body(): weighted, coverage = lax.psum((weighted, coverage), 'visit')  54.8 us
    another operation x1, loops' own time, body(): lax.fori_loop(0, buffer_slots, place_block, (empty, empty))  31.4 us
    gather x24, local copies, waits for them, and re-layouts  20.8 us
    dynamic_update_slice x8, local copies, waits for them, and re-layouts, place_block(): lax.dynamic_update_slice(weighted, region + block_weight * arrived[positi...  14.4 us
    dynamic_update_slice x8, local copies, waits for them, and re-layouts, place_block(): lax.dynamic_update_slice(coverage, region + block_weight, (corner_top, co...  14.4 us
    all_to_all x1, waiting for transfers between devices, body(): lax.all_to_all(cut_back, 'sky', split_axis=0, concat_axis=0, tiled=True)  13.7 us
    add x8, other arithmetic, place_block(): region + block_weight * arrived[position]  6.03 us
    ppermute x3, starting transfers between devices, compute_columns(): lax.ppermute(item_now, axis_name=ax_name, perm=list(map(lambda jj: (jj, j...  5.71 us
  transfers between devices with their start and end apart: 7, of which 4 were waited for; matrix products, arithmetic and copies ran while one was open for 1% of the time, Pallas kernels for 0%

profile of v1, /device:TPU:0, one launch (start us, length us, event | category | flops | bytes accessed | tf_op | source)
XLA Modules:
  0.0 261.7 jit_solution(1871796020282940721)
XLA Ops:
  7.8 0.7 multiply_reduce_fusion.5
  10.4 0.7 multiply_reduce_fusion.1
  17.1 0.7 stack.2
  17.9 0.9 copy-done.4
  18.8 15.7 %while.42 = (s32[]{:T(128)}, f32[4,128,128]{2,1,0:T(8,128)S(1)}, f32[4,3,49]{2,1,0:T(4,128)S(1)}, f32[7,128,128]{2,0,1:T(8,128)S(1)}, f32[4,128,128]{2,1,0:T(8,128)S(1)}, /*index=5*/s32[]{:T(128)}) while((s32[]{:T(128)}, f32[4,128,128]{2,1,0:T(8,128)S(1)}, f32[4,3,49]{2,1,0:T(4,128)S(1)}, ...), condition=%wide.region_10.11_spmd.clone.clone, body=%wide.region_9.10_spmd.clone.clone.sunk | while | flops 557646336 | bytes 6362725 | solution.py:86
  20.1 0.7 convolution_bitcast_fusion.10
  24.1 0.7 convolution_bitcast_fusion.10
  28.0 0.7 convolution_bitcast_fusion.10
  32.0 0.7 convolution_bitcast_fusion.10
  37.1 3.1 %collective-permute-start = (f32[2,128,128]{2,0,1:T(2,128)S(1)}, f32[2,128,128]{2,0,1:T(2,128)S(1)}, u32[]{:S(2)}, u32[]{:S(2)}) collective-permute-start(f32[2,128,128]{2,0,1:T(2,128)S(1)} %get-tuple-element.331), channel_id=1, source_target_pairs={{0,1},{1,0},{2,3},{3,2},{4,5},{5,4},{6,7},{7,6},{8,9},{9,8},{10,11... | collective-permute-start | bytes 393224 | tf_op jit(solution)/shard_map/ppermute | solution.py:26
  40.2 2.6 collective-permute-start.1
  43.0 0.7 copy.69
  43.7 5.1 %all-to-all-start.1 = ((f32[4,2,1]{1,2,0:T(1,128)}), f32[4,2,1]{1,2,0:T(1,128)S(1)}, u32[]{:S(2)}, u32[]{:S(2)}) async-start(f32[4,2,1]{1,2,0:T(1,128)} %copy.69), calls=%async_computation.1 | async-start | bytes 4096 | tf_op jit(solution)/shard_map/all_to_all | solution.py:103
  49.5 0.7 fusion.28
  50.3 4.3 %all-to-all-done.1 = f32[4,2,1]{1,2,0:T(1,128)S(1)} async-done(((f32[4,2,1]{1,2,0:T(1,128)}), f32[4,2,1]{1,2,0:T(1,128)S(1)}, u32[]{:S(2)}, u32[]{:S(2)}) %all-to-all-start.1) | async-done | bytes 64 | tf_op jit(solution)/shard_map/all_to_all | solution.py:103
  54.6 3.7 %all-to-all-start = ((f32[4,2,2]{2,1,0:T(2,128)}), f32[4,2,2]{2,1,0:T(2,128)S(1)}, u32[]{:S(2)}, u32[]{:S(2)}) async-start(f32[4,2,2]{2,1,0:T(2,128)} %fusion.28), calls=%async_computation | async-start | bytes 8192 | tf_op jit(solution)/shard_map/all_to_all | solution.py:104
  58.8 0.7 reduce.27
  59.6 4.3 %all-to-all-done = f32[4,2,2]{2,1,0:T(2,128)S(1)} async-done(((f32[4,2,2]{2,1,0:T(2,128)}), f32[4,2,2]{2,1,0:T(2,128)S(1)}, u32[]{:S(2)}, u32[]{:S(2)}) %all-to-all-start) | async-done | bytes 96 | tf_op jit(solution)/shard_map/all_to_all | solution.py:104
  64.3 75.6 %while.40 = (s32[]{:T(128)}, f32[256,256]{1,0:T(8,128)S(1)}, f32[256,256]{1,0:T(8,128)S(1)}, s32[8,2]{0,1:T(2,128)S(1)}, f32[8]{0:T(128)S(1)}, /*index=5*/f32[8,...) while((s32[]{:T(128)}, f32[256,256]{1,0:T(8,128)S(1)}, f32[256,256]{1,0:T(8,128)S(1)}, ...), condition=%wide.region_12.13_spmd, body=%wide.region_11.12_spmd.sunk | while | flops 49160 | bytes 591569 | solution.py:124
  69.4 0.8 bitcast_add_fusion.2
  70.2 2.0 dynamic_update_slice.52
  72.1 2.0 dynamic_update_slice.51
  79.2 0.8 bitcast_add_fusion.2
  80.0 1.9 dynamic_update_slice.52
  81.9 1.9 dynamic_update_slice.51
  88.9 0.8 bitcast_add_fusion.2
  89.7 2.0 dynamic_update_slice.52
  91.7 2.0 dynamic_update_slice.51
  98.7 0.8 bitcast_add_fusion.2
  99.5 1.7 dynamic_update_slice.52
  101.2 1.7 dynamic_update_slice.51
  107.9 0.8 bitcast_add_fusion.2
  108.7 1.9 dynamic_update_slice.52
  110.6 1.9 dynamic_update_slice.51
  117.5 0.8 bitcast_add_fusion.2
  118.3 1.7 dynamic_update_slice.52
  119.9 1.7 dynamic_update_slice.51
  126.7 0.8 bitcast_add_fusion.2
  127.5 1.7 dynamic_update_slice.52
  129.1 1.7 dynamic_update_slice.51
  135.9 0.8 bitcast_add_fusion.2
  136.6 1.7 dynamic_update_slice.52
  138.3 1.7 dynamic_update_slice.51
  140.0 0.7 copy-done.1
  140.8 54.8 %all-reduce.3.cloned.1.call-done = (f32[256,256]{1,0:T(8,128)}, f32[256,256]{1,0:T(8,128)}) async-done(((f32[256,256]{1,0:T(8,128)}, f32[256,256]{1,0:T(8,128)}), (f32[256,256]{1,0:T(8,128)}, f32[256,256]{1,0:T(8,128)})) %all-reduce.3.cloned.1.call-update) | async-done | bytes 524304 | tf_op jit(solution)/shard_map/psum | solution.py:125
  195.6 1.1 add_divide_fusion
  196.7 0.8 broadcast_in_dim.77
  197.5 20.8 %while.41 = (s32[]{:T(128)}, f32[256,256]{1,0:T(8,128)S(1)}, s32[8,2]{0,1:T(2,128)S(1)}, f32[8,128,128]{2,1,0:T(8,128)}, s32[]{:T(128)}) while((s32[]{:T(128)}, f32[256,256]{1,0:T(8,128)S(1)}, s32[8,2]{0,1:T(2,128)S(1)}, f32[8,128,128]{2,1,0:T(8,128)}, s32[]{:T(128)}) %tuple.119), condition=%wide.while_cond, body=%wide.while_body.sunk | while | flops 2 | bytes 132705 | solution.py:128
  198.1 2.0 bitcast_dynamic-update-slice_fusion.2
  200.7 2.0 bitcast_dynamic-update-slice_fusion.2
  203.3 2.0 bitcast_dynamic-update-slice_fusion.2
  205.9 2.0 bitcast_dynamic-update-slice_fusion.2
  208.5 2.0 bitcast_dynamic-update-slice_fusion.2
  211.1 2.0 bitcast_dynamic-update-slice_fusion.2
  213.7 2.0 bitcast_dynamic-update-slice_fusion.2
  216.3 2.0 bitcast_dynamic-update-slice_fusion.2
  218.3 0.7 copy-done.3
  219.0 4.6 %all-to-all-start.2 = ((f32[8,128,128]{2,1,0:T(8,128)}), f32[8,128,128]{2,1,0:T(8,128)S(1)}, u32[]{:S(2)}, u32[]{:S(2)}) async-start(f32[8,128,128]{2,1,0:T(8,128)} %get-tuple-element.193), calls=%async_computation.2 | async-start | bytes 1048576 | tf_op jit(solution)/shard_map/all_to_all | solution.py:130
  223.6 13.7 %all-to-all-done.2 = f32[8,128,128]{2,1,0:T(8,128)S(1)} async-done(((f32[8,128,128]{2,1,0:T(8,128)}), f32[8,128,128]{2,1,0:T(8,128)S(1)}, u32[]{:S(2)}, u32[]{:S(2)}) %all-to-all-start.2) | async-done | bytes 524320 | tf_op jit(solution)/shard_map/all_to_all | solution.py:130
  237.3 0.7 fusion.23
  238.0 16.0 %while.43 = (s32[]{:T(128)}, f32[4,128,128]{2,1,0:T(8,128)S(1)}, f32[4,3,49]{2,1,0:T(4,128)S(1)}, f32[7,128,128]{2,0,1:T(8,128)S(1)}, f32[4,128,128]{2,0,1:T(4,128)S(1)}, /*index=5*/s32[]{:T(128)}) while((s32[]{:T(128)}, f32[4,128,128]{2,1,0:T(8,128)S(1)}, f32[4,3,49]{2,1,0:T(4,128)S(1)}, ...), condition=%wide.region_16.17_spmd.clone.clone, body=%wide.region_15.16_spmd.clone.clone.sunk | while | flops 557646336 | bytes 6428261 | solution.py:134
  243.5 0.6 convolution_bitcast_fusion.12
  247.5 0.6 convolution_bitcast_fusion.12
  254.1 0.8 select_bitcast_fusion
  (184 shorter events, 49.2 us)
Async XLA Ops:
  7.2 35.7 %copy-start = (f32[1,4]{1,0:T(1,128)S(1)}, f32[1,4]{1,0:T(1,128)}, u32[]{:S(2)}) copy-start(f32[1,4]{1,0:T(1,128)} %param.17) | copy-start | bytes 52
  12.3 4.1 %copy-start.5 = (f32[1,4,3,49]{3,1,2,0:T(4,128)S(1)}, f32[1,4,3,49]{3,1,2,0:T(4,128)}, u32[]{:S(2)}) copy-start(f32[1,4,3,49]{3,1,2,0:T(4,128)} %param.15) | copy-start | bytes 7060
  17.8 1.0 copy-start.4
  35.2 0.7 copy-start.8
  35.2 0.7 copy-start.9
  37.1 27.1 %collective-permute-start = (f32[2,128,128]{2,0,1:T(2,128)S(1)}, f32[2,128,128]{2,0,1:T(2,128)S(1)}, u32[]{:S(2)}, u32[]{:S(2)}) collective-permute-start(f32[2,128,128]{2,0,1:T(2,128)S(1)} %get-tuple-element.331), channel_id=1, source_target_pairs={{0,1},{1,0},{2,3},{3,2},{4,5},{5,4},{6,7},{7,6},{8,9},{9,8},{10,11... | collective-permute-start | bytes 393224 | tf_op jit(solution)/shard_map/ppermute | solution.py:26
  40.2 24.0 %collective-permute-start.1 = (f32[2,128,128]{2,0,1:T(2,128)S(1)}, f32[2,128,128]{2,0,1:T(2,128)S(1)}, u32[]{:S(2)}, u32[]{:S(2)}) collective-permute-start(f32[2,128,128]{2,0,1:T(2,128)S(1)} %get-tuple-element.330), channel_id=1, source_target_pairs={{0,2},{1,3},{2,0},{3,1},{4,6},{5,7},{6,4},{7,5},{8,10},{9,11},{10,... | collective-permute-start | bytes 393224 | tf_op jit(solution)/shard_map/ppermute | solution.py:26
  42.8 21.5 %collective-permute-start.2 = (f32[2,128,128]{2,0,1:T(2,128)S(1)}, f32[2,128,128]{2,0,1:T(2,128)S(1)}, u32[]{:S(2)}, u32[]{:S(2)}) collective-permute-start(f32[2,128,128]{2,0,1:T(2,128)S(1)} %get-tuple-element.329), channel_id=1, source_target_pairs={{0,3},{1,2},{2,1},{3,0},{4,7},{5,6},{6,5},{7,4},{8,11},{9,10},{10,... | collective-permute-start | bytes 393224 | tf_op jit(solution)/shard_map/ppermute | solution.py:26
  43.7 10.8 %all-to-all-start.1 = ((f32[4,2,1]{1,2,0:T(1,128)}), f32[4,2,1]{1,2,0:T(1,128)S(1)}, u32[]{:S(2)}, u32[]{:S(2)}) async-start(f32[4,2,1]{1,2,0:T(1,128)} %copy.69), calls=%async_computation.1 | async-start | bytes 4096 | tf_op jit(solution)/shard_map/all_to_all | solution.py:103
  48.9 0.7 copy-start.7
  54.6 9.3 %all-to-all-start = ((f32[4,2,2]{2,1,0:T(2,128)}), f32[4,2,2]{2,1,0:T(2,128)S(1)}, u32[]{:S(2)}, u32[]{:S(2)}) async-start(f32[4,2,2]{2,1,0:T(2,128)} %fusion.28), calls=%async_computation | async-start | bytes 8192 | tf_op jit(solution)/shard_map/all_to_all | solution.py:104
  58.3 137.3 %all-reduce.3.cloned.1.call-start = ((), (), s32[]{:S(2)}) async-start(), calls=%async_computation.3 | async-start | bytes 1048576 | tf_op jit(solution)/shard_map/psum | solution.py:125
  140.0 0.7 copy-start.1
  140.0 0.8 copy-start.2
  218.3 0.7 copy-start.3
  218.3 5.3 %copy-start.6 = (f32[1,4,3,49]{3,1,2,0:T(4,128)S(1)}, f32[1,4,3,49]{3,1,2,0:T(4,128)}, u32[]{:S(2)}) copy-start(f32[1,4,3,49]{3,1,2,0:T(4,128)} %param.16) | copy-start | bytes 7060
  219.0 18.3 %all-to-all-start.2 = ((f32[8,128,128]{2,1,0:T(8,128)}), f32[8,128,128]{2,1,0:T(8,128)S(1)}, u32[]{:S(2)}, u32[]{:S(2)}) async-start(f32[8,128,128]{2,1,0:T(8,128)} %get-tuple-element.193), calls=%async_computation.2 | async-start | bytes 1048576 | tf_op jit(solution)/shard_map/all_to_all | solution.py:130
Sparse Core Ops, SparseCore 0:
  140.9 54.6 all-reduce.2
